TPU v7x, 32 devices: a whole 2x2x4 slice. The times are simulated.
32 devices in a mesh: grp: 2 (over y), slab: 4 (over z), head: 2 (over x), seq: 2 (over core).
Axes of the slice: x: 2, y: 2, z: 4, core: 2. Of those that a mesh axis runs over, the one named last changes fastest.
Arguments:
- queries: bfloat16 [1024, 5120], P(('grp', 'seq'), 'head'), parts along dimension 0, may hold values from -140 to 140
- query_gain: float32 [5120], P('head'), may hold values from 1.5 to 3
- cache_keys: bfloat16 [4096, 5120], P(('grp', 'slab'), 'head'), parts along dimension 0, may hold values from -120 to 120
- cache_values: bfloat16 [4096, 5120], P(('grp', 'slab'), 'head'), parts along dimension 0, may hold values from -6 to 6
- finished_keys: bfloat16 [1024, 5120], P(('grp', 'slab', 'seq'), 'head'), parts along dimension 0, may hold values from -6 to 6
- finished_values: bfloat16 [1024, 5120], P(('grp', 'slab', 'seq'), 'head'), parts along dimension 0, may hold values from -6 to 6
- new_keys: bfloat16 [1024, 5120], P(('grp', 'slab', 'seq'), 'head'), parts along dimension 0, may hold values from -6 to 6
- new_values: bfloat16 [1024, 5120], P(('grp', 'slab', 'seq'), 'head'), parts along dimension 0, may hold values from -6 to 6
- out_weight: bfloat16 [5120, 5120], P('head', 'slab'), may hold values from -0.25 to 0.25
- time_weight: float32 [256, 5120], P(None, ('slab', 'head')), may hold values from -0.375 to 0.375
- owner: int32 [2], P('grp'), parts along dimension 0, may hold values from 0 to 3
- step: int32 [2], P('grp'), parts along dimension 0, may hold values from 0 to 999
Outputs:
- branch: bfloat16 [1024, 5120], P(('grp', 'seq'), ('slab', 'head')), parts along dimension 0
There are 2 independent parts, one for each index of `grp`. A program takes and returns all parts, laid end to end along the dimension named above; an argument that names none is the same for every part. Nothing has to cross between parts.
All inputs are finite; a program needn't handle non-finite values.
Results may differ from a plain program's by a relative error of at most 0.012.
Values may be sent and summed in bfloat16 or wider, within the bound.
No kernel may reach another device: no remote copies, remote signals or barrier semaphores. Data moves between devices by JAX's collectives and lax.ppermute only.
A program may use at most 64 MiB of HBM per device.

v0:
```python
from functools import reduce
import jax
import jax.numpy as jnp
from jax import lax
from jax.sharding import PartitionSpec as P

HEADS = 40
HD = 128
EPSILON = 1e-06


def local(
    queries,
    query_gain,
    cache_keys,
    cache_values,
    finished_keys,
    finished_values,
    new_keys,
    new_values,
    out_weight,
    time_weight,
    owner,
    step,
):
    row_count = queries.shape[0]
    head_count = queries.shape[1] // HD
    query_float = queries.astype(jnp.float32)
    norm_total = lax.psum(jnp.sum(query_float * query_float, axis=1), "head")
    inverse = lax.rsqrt(norm_total / (HEADS * HD) + EPSILON)
    normed = (
        (query_float * inverse[:, None] * query_gain)
        .astype(jnp.bfloat16)
        .reshape(row_count, head_count, HD)
    )
    is_owner = lax.axis_index("slab") == owner[0]
    whole_keys, whole_values = (
        lax.all_gather(finished_keys, ("slab", "seq"), axis=0, tiled=True),
        lax.all_gather(finished_values, ("slab", "seq"), axis=0, tiled=True),
    )
    fresh_keys, fresh_values = (
        lax.all_gather(new_keys, "seq", axis=0, tiled=True),
        lax.all_gather(new_values, "seq", axis=0, tiled=True),
    )
    key_block = jnp.where(is_owner, whole_keys, cache_keys)
    value_block = jnp.where(is_owner, whole_values, cache_values)
    blocks = [
        (key_block, value_block, jnp.float32(0.0)),
        (fresh_keys, fresh_values, jnp.float32(0.0)),
    ]
    score_scale = 1.0 / HD**0.5
    score_list = []
    for key_block, value_block, penalty in blocks:
        key_heads = key_block.reshape(key_block.shape[0], head_count, HD)
        each_score = jnp.einsum(
            "rhd,khd->hrk", normed, key_heads, preferred_element_type=jnp.float32
        )
        score_list.append(each_score * score_scale)
    row_top = reduce(jnp.maximum, [jnp.max(each_score, axis=2) for each_score in score_list])
    row_mass = jnp.zeros_like(row_top)
    partial_value = jnp.zeros((head_count, row_count, HD), jnp.float32)
    for each_score, (key_block, value_block, penalty) in zip(score_list, blocks):
        raw_weights = jnp.exp(each_score - row_top[:, :, None])
        row_mass = row_mass + jnp.sum(raw_weights, axis=2)
        value_heads = value_block.reshape(value_block.shape[0], head_count, HD)
        partial_value = partial_value + jnp.einsum(
            "hrk,khd->hrd",
            raw_weights.astype(jnp.bfloat16),
            value_heads,
            preferred_element_type=jnp.float32,
        )
    global_top = lax.pmax(row_top, "slab")
    factor = jnp.exp(row_top - global_top)
    sum_share, mass_share = (
        lax.psum_scatter(
            partial_value * factor[:, :, None], "slab", scatter_dimension=1, tiled=True
        ),
        lax.psum_scatter(row_mass * factor, "slab", scatter_dimension=1, tiled=True),
    )
    row_share = (sum_share / mass_share[:, :, None]).astype(jnp.bfloat16)
    attended = lax.all_gather(row_share, "slab", axis=1, tiled=True)
    weight_heads = out_weight.reshape(head_count, HD, out_weight.shape[1])
    projected = jnp.einsum(
        "hrd,hdc->rc", attended, weight_heads, preferred_element_type=jnp.float32
    )
    summed = lax.psum_scatter(projected, "head", scatter_dimension=1, tiled=True)
    half = time_weight.shape[0] // 2
    frequency = jnp.exp(-jnp.log(10000.0) * jnp.arange(half, dtype=jnp.float32) / half)
    phases = step[0].astype(jnp.float32) * frequency
    embedding = jnp.concatenate([jnp.cos(phases), jnp.sin(phases)])
    time_gate = 1.0 + jnp.dot(embedding, time_weight, precision=lax.Precision.HIGHEST)
    return (time_gate * summed).astype(jnp.bfloat16)


def solution(mesh):
    in_specs = (
        P(("grp", "seq"), "head"),
        P("head"),
        P(("grp", "slab"), "head"),
        P(("grp", "slab"), "head"),
        P(("grp", "slab", "seq"), "head"),
        P(("grp", "slab", "seq"), "head"),
        P(("grp", "slab", "seq"), "head"),
        P(("grp", "slab", "seq"), "head"),
        P("head", "slab"),
        P(None, ("slab", "head")),
        P("grp"),
        P("grp"),
    )
    out_specs = P(("grp", "seq"), ("slab", "head"))
    return jax.shard_map(local, mesh=mesh, in_specs=in_specs, out_specs=out_specs, check_vma=False)
```

profile of v0, /device:TPU:0, one launch (start us, length us, event | category | flops | bytes accessed | tf_op | source)
XLA Modules:
  0.0 240.0 jit_solution(8406601955525841598)
XLA Ops:
  6.5 0.7 all-gather.4.cloned.1.call-update
  7.3 0.0 all-gather.6.cloned.1.call-start
  7.3 0.7 all-gather.6.cloned.1.call-update
  8.0 0.0 reduce-scatter.10.cloned.1.call-start
  8.1 4.5 %copy.36 = bf16[512,2560]{0,1:T(8,128)(2,1)} copy(bf16[512,2560]{1,0:T(8,128)(2,1)} %param.15) | data formatting | bytes 5242880 | tf_op args[3]
  13.3 0.0 copy-done.3
  13.3 0.6 copy.27
  13.9 0.0 copy-start.4
  13.9 0.0 copy-start.5
  13.9 4.5 %copy.29 = bf16[512,2560]{0,1:T(8,128)(2,1)} copy(bf16[512,2560]{1,0:T(8,128)(2,1)} %param.14) | data formatting | bytes 5242880 | tf_op args[2]
  18.4 2.7 %all_gather.16 = bf16[128,2560]{1,0:T(8,128)(2,1)S(1)} all-gather(bf16[64,2560]{1,0:T(8,128)(2,1)S(1)} %copy-done.4), channel_id=1, replica_groups=mesh['grp'=2,'slab'=4,'head'=2,'seq'=2] {'seq'}, dimensions={0}, use_global_device_ids=true | all-gather | bytes 983040 | tf_op jit(solution)/shard_map/all_gather | solution.py:42
  21.1 1.1 copy.32
  22.2 2.3 all_gather.18
  24.4 1.1 copy.38
  25.5 0.4 fusion.6
  25.9 5.5 %psum.7 = f32[256]{0:T(256)S(1)} all-reduce(f32[256]{0:T(256)S(1)} %fusion.6), channel_id=1, replica_groups=mesh['grp'=2,'slab'=4,'head'=2,'seq'=2] {'head'}, use_global_device_ids=true, to_apply=%region_1.0 | all-reduce | flops 256 | bytes 2048 | tf_op jit(solution)/shard_map/psum | solution.py:29
  31.5 0.4 fusion.8
  31.9 1.2 copy-done.1
  33.0 1.7 multiply_reduce_fusion.1
  34.7 10.7 %all-gather.4.cloned.1.call-done = bf16[512,2560]{1,0:T(8,128)(2,1)} async-done(((bf16[64,2560]{1,0:T(8,128)(2,1)}), bf16[512,2560]{1,0:T(8,128)(2,1)}) %all-gather.4.cloned.1.call-update) | async-done | bytes 2621456 | tf_op jit(solution)/shard_map/all_gather | solution.py:38
  45.4 4.4 %copy.28 = bf16[512,2560]{0,1:T(8,128)(2,1)} copy(bf16[512,2560]{1,0:T(8,128)(2,1)} %all-gather.4.cloned.1.call-done) | data formatting | bytes 5242880 | tf_op jit(solution)/shard_map/all_gather | solution.py:38
  49.8 2.1 broadcast_select_fusion.1
  52.0 5.7 %multiply_reduce_fusion = (f32[20,256]{1,0:T(8,128)S(1)}, f32[20,256,512]{2,1,0:T(8,128)}) fusion(bf16[256,20,128]{0,2,1:T(8,128)(2,1)S(1)} %bitcast.25, bf16[512,20,128]{0,2,1:T(8,128)(2,1)S(1)} %bitcast.27), kind=kOutput, calls=%fused_computation.1 | convolution fusion | flops 676326400 | bytes 14438400 | tf_op jit(solution)/shard_map/rhd,khd->hrk/dot_general | solution.py:55
  57.6 18.7 %pmax.7 = f32[20,256]{1,0:T(8,128)S(1)} all-reduce(f32[20,256]{1,0:T(8,128)S(1)} %max.9), channel_id=1, replica_groups=mesh['grp'=2,'slab'=4,'head'=2,'seq'=2] {'slab'}, use_global_device_ids=true, to_apply=%region_4.5 | all-reduce | flops 5120 | bytes 40960 | tf_op jit(solution)/shard_map/pmax | solution.py:72
  76.4 5.9 %fusion = f32[20,256]{1,0:T(8,128)S(1)} fusion(f32[20,256,512]{2,1,0:T(8,128)} %get-tuple-element.8, f32[20,256]{1,0:T(8,128)S(1)} %max.9), kind=kLoop, calls=%fused_computation.2 | loop fusion | flops 7859200 | bytes 10526720 | tf_op jit(solution)/shard_map/reduce_sum | solution.py:64
  82.2 0.0 all-gather.6.cloned.1.call-done
  82.3 4.4 %copy.35 = bf16[512,2560]{0,1:T(8,128)(2,1)} copy(bf16[512,2560]{1,0:T(8,128)(2,1)} %all-gather.6.cloned.1.call-done) | data formatting | bytes 5242880 | tf_op jit(solution)/shard_map/all_gather | solution.py:39
  86.7 2.0 broadcast_select_fusion
  88.7 7.7 %fusion.2 = f32[20,256,128]{2,1,0:T(8,128)} fusion(bf16[512,20,128]{0,2,1:T(8,128)(2,1)S(1)} %bitcast.26, f32[20,256,512]{2,1,0:T(8,128)} %get-tuple-element.8, f32[20,256]{1,0:T(8,128)S(1)} %max.9), kind=kOutput, calls=%fused_computation.4 | convolution fusion | flops 678952960 | bytes 15749120 | tf_op jit(solution)/shard_map/hrk,khd->hrd/dot_general | solution.py:66
  96.4 0.5 fusion.9
  96.9 0.8 copy.48
  97.6 0.0 reduce-scatter.10.cloned.1.call-update
  97.7 0.0 reduce-scatter.6.cloned.1.call-start
  97.7 4.1 %add_multiply_fusion = f32[20,256,128]{2,1,0:T(8,128)} fusion(f32[20,256,128]{2,1,0:T(8,128)} %fusion.2, bf16[128,20,128]{0,2,1:T(8,128)(2,1)} %bitcast.28, f32[20,256,128]{1,2,0:T(8,128)S(1)} %get-tuple-element.10, f32[20,256]{1,0:T(8,128)S(1)} %get-tuple-element.6, f32[20,256]{1,0:T(8,128)S(1)} %max.9), kind=kOutput, calls=%fused_computation.13 | convolution fusion | flops 171048960 | bytes 8560640 | tf_op jit(solution)/shard_map/hrk,khd->hrd/dot_general | solution.py:66
  101.8 0.0 reduce-scatter.6.cloned.1.call-update
  101.8 0.0 all-gather.8.cloned.1.call-start
  101.9 13.7 %reduce-scatter.10.cloned.1.call-done = f32[64,20]{1,0:T(8,128)} async-done(((f32[256,20]{1,0:T(8,128)}), f32[64,20]{1,0:T(8,128)}) %reduce-scatter.10.cloned.1.call-update) | async-done | bytes 5136
  115.6 0.8 copy.49
  116.4 51.8 %reduce-scatter.6.cloned.1.call-done = f32[20,64,128]{2,1,0:T(8,128)} async-done(((f32[20,256,128]{2,1,0:T(8,128)}), f32[20,64,128]{2,1,0:T(8,128)}) %reduce-scatter.6.cloned.1.call-update) | async-done | bytes 655376 | tf_op jit(solution)/shard_map/reduce_scatter | solution.py:75
  168.2 2.1 divide_convert_fusion
  170.3 0.0 all-gather.8.cloned.1.call-update
  170.3 0.0 reduce-scatter.8.cloned.1.call-start
  170.4 32.2 %all-gather.8.cloned.1.call-done = bf16[20,256,128]{2,1,0:T(8,128)(2,1)} async-done(((bf16[20,64,128]{2,1,0:T(8,128)(2,1)}), bf16[20,256,128]{2,1,0:T(8,128)(2,1)}) %all-gather.8.cloned.1.call-update) | async-done | bytes 1310736 | tf_op jit(solution)/shard_map/all_gather | solution.py:81
  202.5 6.2 %convolution_bitcast_fusion = f32[256,1280]{1,0:T(8,128)} fusion(bf16[20,256,128]{2,1,0:T(8,128)(2,1)} %all-gather.8.cloned.1.call-done, bf16[20,128,1280]{2,1,0:T(8,128)(2,1)} %bitcast.33), kind=kOutput, calls=%fused_computation.9 | convolution fusion | flops 1677721600 | bytes 9175040 | tf_op jit(solution)/shard_map/hrd,hdc->rc/dot_general | solution.py:83
  208.7 0.0 reduce-scatter.8.cloned.1.call-update
  209.5 0.4 convolution_reduce_fusion
  209.9 21.4 %reduce-scatter.8.cloned.1.call-done = f32[256,640]{1,0:T(8,128)} async-done(((f32[256,1280]{1,0:T(8,128)}), f32[256,640]{1,0:T(8,128)}) %reduce-scatter.8.cloned.1.call-update) | async-done | bytes 655376 | tf_op jit(solution)/shard_map/reduce_scatter | solution.py:86
  231.3 1.9 multiply_convert_fusion
  (17 shorter events, 0.1 us)
Async XLA Ops:
  6.5 202.9 %copy-start = (f32[256,640]{1,0:T(8,128)S(1)}, f32[256,640]{1,0:T(8,128)}, u32[]{:S(2)}) copy-start(f32[256,640]{1,0:T(8,128)} %param.21) | copy-start | bytes 1966084
  6.5 38.9 %all-gather.4.cloned.1.call-start = ((), (), s32[]{:S(2)}) async-start(), calls=%async_computation.3 | async-start | bytes 2949120 | tf_op jit(solution)/shard_map/all_gather | solution.py:38
  7.3 75.0 %all-gather.6.cloned.1.call-start = ((), (), s32[]{:S(2)}) async-start(), calls=%async_computation.4 | async-start | bytes 2949120 | tf_op jit(solution)/shard_map/all_gather | solution.py:39
  8.0 107.6 %reduce-scatter.10.cloned.1.call-start = ((), (), s32[]{:S(2)}) async-start(), calls=%async_computation.8 | async-start | bytes 163840
  8.1 5.2 %copy-start.3 = (bf16[256,2560]{1,0:T(8,128)(2,1)S(1)}, bf16[256,2560]{1,0:T(8,128)(2,1)}, u32[]{:S(2)}) copy-start(bf16[256,2560]{1,0:T(8,128)(2,1)} %param.12) | copy-start | bytes 3932164
  13.9 4.5 %copy-start.4 = (bf16[64,2560]{1,0:T(8,128)(2,1)S(1)}, bf16[64,2560]{1,0:T(8,128)(2,1)}, u32[]{:S(2)}) copy-start(bf16[64,2560]{1,0:T(8,128)(2,1)} %param.18) | copy-start | bytes 983044
  13.9 8.3 %copy-start.5 = (bf16[64,2560]{1,0:T(8,128)(2,1)S(1)}, bf16[64,2560]{1,0:T(8,128)(2,1)}, u32[]{:S(2)}) copy-start(bf16[64,2560]{1,0:T(8,128)(2,1)} %param.19) | copy-start | bytes 983044
  21.1 10.4 %copy-start.6 = (f32[2560]{0:T(1024)S(1)}, f32[2560]{0:T(1024)}, u32[]{:S(2)}) copy-start(f32[2560]{0:T(1024)} %param.13) | copy-start | bytes 30724
  31.9 1.2 copy-start.1
  49.8 2.1 copy-start.2
  97.7 70.6 %reduce-scatter.6.cloned.1.call-start = ((), (), s32[]{:S(2)}) async-start(), calls=%async_computation.5 | async-start | bytes 3276800 | tf_op jit(solution)/shard_map/reduce_scatter | solution.py:75
  101.8 100.7 %all-gather.8.cloned.1.call-start = ((), (), s32[]{:S(2)}) async-start(), calls=%async_computation.6 | async-start | bytes 1638400 | tf_op jit(solution)/shard_map/all_gather | solution.py:81
  170.3 61.0 %reduce-scatter.8.cloned.1.call-start = ((), (), s32[]{:S(2)}) async-start(), calls=%async_computation.7 | async-start | bytes 1966080 | tf_op jit(solution)/shard_map/reduce_scatter | solution.py:86
Sparse Core Ops, SparseCore 0:
  9.0 36.4 all-gather.3
  47.1 33.8 all-gather.5
  97.8 17.7 reduce-scatter.9
  117.7 50.4 reduce-scatter.5
  170.4 32.0 all-gather.7
  208.9 22.3 reduce-scatter.7
where the time goes:
time: 241 us; the launch traced here: 240 us
  waiting for transfers between devices  131 us (54%)
  blocking collectives  29.2 us (12%)
  matrix products  25.7 us (11%)
  local copies, waits for them, and re-layouts  23.4 us (10%)
  other arithmetic  15.2 us (6%)
  between operations  14.9 us (6%)
    reduce_scatter x1, waiting for transfers between devices, local(): lax.psum_scatter(partial_value * factor[:, :, None], 'slab', scatter_dime...  51.8 us
    all_gather x1, waiting for transfers between devices, local(): attended = lax.all_gather(row_share, 'slab', axis=1, tiled=True)  32.2 us
    reduce_scatter x1, waiting for transfers between devices, local(): lax.psum_scatter(projected, 'head', scatter_dimension=1, tiled=True)  21.4 us
    pmax x1, blocking collectives, local(): global_top = lax.pmax(row_top, 'slab')  18.7 us
    unnamed x7, waiting for transfers between devices  15.2 us
    unnamed x19, local copies, waits for them, and re-layouts  12.4 us
    dot_general x2, matrix products, local(): jnp.einsum('hrk,khd->hrd', raw_weights.astype(jnp.bfloat16), value_heads,...  11.8 us
    all_gather x1, waiting for transfers between devices, local(): lax.all_gather(finished_keys, ('slab', 'seq'), axis=0, tiled=True)  10.7 us
  transfers between devices with their start and end apart: 6, of which 5 were waited for; matrix products, arithmetic and copies ran while one was open for 16% of the time, Pallas kernels for 0%

commit v1 on v0

--- a/solution.py
+++ b/solution.py
@@ -7,6 +7,18 @@
 HEADS = 40
 HD = 128
 EPSILON = 1e-06
+
+
+def doubled_up(x, axis, dim):
+    ways, here, turn = (lax.axis_size(axis), lax.axis_index(axis), x.shape[dim])
+    line, have = (x, 1)
+    while have < ways:
+        line = jnp.concatenate(
+            [line, lax.ppermute(line, axis, [(d, (d - have) % ways) for d in range(ways)])],
+            axis=dim,
+        )
+        have = 2 * have
+    return jnp.roll(line, here * turn, axis=dim)
 
 
 def local(
@@ -35,7 +47,7 @@
     )
     is_owner = lax.axis_index("slab") == owner[0]
     whole_keys, whole_values = (
-        lax.all_gather(finished_keys, ("slab", "seq"), axis=0, tiled=True),
+        doubled_up(finished_keys, ("slab", "seq"), 0),
         lax.all_gather(finished_values, ("slab", "seq"), axis=0, tiled=True),
     )
     fresh_keys, fresh_values = (

time: 241 us -> 303 us (1.26)
  waiting for transfers between devices: 131 us -> 169 us
  local copies, waits for them, and re-layouts: 23.4 us -> 33.6 us
  blocking collectives: 29.2 us -> 35.9 us
  starting transfers between devices: 0.2 us -> 5.51 us
  other arithmetic: 15.2 us -> 20.4 us
  matrix products: 25.7 us -> 20.7 us
    ppermute x0 -> x3, waiting for transfers between devices: none -> 60.4 us  [doubled_up(): lax.ppermute(line, axis, [(d, (d - have) % ways) for d in range(ways)])]
    unnamed x7 -> x6, waiting for transfers between devices: 15.2 us -> 3.27 us
    all_gather x1 -> x0, waiting for transfers between devices: 10.7 us -> none  [local(): lax.all_gather(finished_keys, ('slab', 'seq'), axis=0, tiled=True)]
    concatenate x0 -> x1, local copies, waits for them, and re-layouts: none -> 9.9 us  [doubled_up(): return jnp.roll(line, here * turn, axis=dim)]
    ppermute x0 -> x3, starting transfers between devices: none -> 5.15 us  [doubled_up(): lax.ppermute(line, axis, [(d, (d - have) % ways) for d in range(ways)])]
    all_gather x1 -> x0, local copies, waits for them, and re-layouts: 4.4 us -> none  [local(): lax.all_gather(finished_keys, ('slab', 'seq'), axis=0, tiled=True)]
    all_gather x1, blocking collectives: 2.68 us -> 6.91 us  [local(): lax.all_gather(new_keys, 'seq', axis=0, tiled=True)]
    dot_general x2, matrix products: 11.8 us -> 7.82 us  [local(): jnp.einsum('hrk,khd->hrd', raw_weights.astype(jnp.bfloat16), value_heads,...]
  transfers between devices with their start and end apart: 6 -> 8, of which waited for: 5 -> 6; matrix products, arithmetic and copies ran while one was open for 16% -> 21% of each run, Pallas kernels for 0% -> 0%
where the time goes in v1:
time: 303 us; the launch traced here: 301 us
  waiting for transfers between devices  169 us (56%)
  blocking collectives  35.9 us (12%)
  local copies, waits for them, and re-layouts  33.6 us (11%)
  matrix products  20.7 us (7%)
  other arithmetic  20.4 us (7%)
  between operations  16.5 us (5%)
  starting transfers between devices  5.51 us (2%)
    ppermute x3, waiting for transfers between devices, doubled_up(): lax.ppermute(line, axis, [(d, (d - have) % ways) for d in range(ways)])  60.4 us
    reduce_scatter x1, waiting for transfers between devices, local(): lax.psum_scatter(partial_value * factor[:, :, None], 'slab', scatter_dime...  51.7 us
    all_gather x1, waiting for transfers between devices, local(): attended = lax.all_gather(row_share, 'slab', axis=1, tiled=True)  31.9 us
    reduce_scatter x1, waiting for transfers between devices, local(): lax.psum_scatter(projected, 'head', scatter_dimension=1, tiled=True)  21.4 us
    pmax x1, blocking collectives, local(): global_top = lax.pmax(row_top, 'slab')  20.1 us
    unnamed x22, local copies, waits for them, and re-layouts  14.6 us
    concatenate x1, local copies, waits for them, and re-layouts, doubled_up(): return jnp.roll(line, here * turn, axis=dim)  9.9 us
    dot_general x2, matrix products, local(): jnp.einsum('hrk,khd->hrd', raw_weights.astype(jnp.bfloat16), value_heads,...  7.82 us
  transfers between devices with their start and end apart: 8, of which 6 were waited for; matrix products, arithmetic and copies ran while one was open for 21% of the time, Pallas kernels for 0%

profile of v1, /device:TPU:0, one launch (start us, length us, event | category | flops | bytes accessed | tf_op | source)
XLA Modules:
  0.0 301.4 jit_solution(14586637500700692597)
XLA Ops:
  7.4 4.5 %collective-permute-start = (bf16[64,2560]{1,0:T(8,128)(2,1)}, bf16[64,2560]{1,0:T(8,128)(2,1)S(1)}, u32[]{:S(2)}, u32[]{:S(2)}) collective-permute-start(bf16[64,2560]{1,0:T(8,128)(2,1)} %param.16), channel_id=1, source_target_pairs={{0,13},{1,0},{4,1},{5,4},{8,5},{9,8},{12,9},{13,12},{2,15},{3,2},{... | collective-permute-start | bytes 983048 | tf_op jit(solution)/shard_map/ppermute | solution.py:17
  11.9 1.3 copy.36
  13.2 3.6 %collective-permute-done = bf16[64,2560]{1,0:T(8,128)(2,1)S(1)} collective-permute-done((bf16[64,2560]{1,0:T(8,128)(2,1)}, bf16[64,2560]{1,0:T(8,128)(2,1)S(1)}, u32[]{:S(2)}, u32[]{:S(2)}) %collective-permute-start) | collective-permute-done | bytes 327712 | tf_op jit(solution)/shard_map/ppermute | solution.py:17
  16.8 0.3 copy.37
  17.1 1.2 pad_maximum_fusion.1
  18.4 0.6 collective-permute-start.1
  19.0 0.0 reduce-scatter.10.cloned.1.call-start
  19.0 4.4 %copy.47 = bf16[512,2560]{0,1:T(8,128)(2,1)} copy(bf16[512,2560]{1,0:T(8,128)(2,1)} %param.15) | data formatting | bytes 5242880 | tf_op args[3]
  24.1 1.6 copy.31
  25.7 4.5 %copy.40 = bf16[512,2560]{0,1:T(8,128)(2,1)} copy(bf16[512,2560]{1,0:T(8,128)(2,1)} %param.14) | data formatting | bytes 5242880 | tf_op args[2]
  30.2 6.9 %all_gather.12 = bf16[128,2560]{1,0:T(8,128)(2,1)} all-gather(bf16[64,2560]{1,0:T(8,128)(2,1)} %param.18), channel_id=1, replica_groups=mesh['grp'=2,'slab'=4,'head'=2,'seq'=2] {'seq'}, dimensions={0}, use_global_device_ids=true | all-gather | bytes 983040 | tf_op jit(solution)/shard_map/all_gather | solution.py:54
  37.1 2.2 copy.43
  39.3 4.0 %all_gather.14 = bf16[128,2560]{1,0:T(8,128)(2,1)} all-gather(bf16[64,2560]{1,0:T(8,128)(2,1)} %param.19), channel_id=1, replica_groups=mesh['grp'=2,'slab'=4,'head'=2,'seq'=2] {'seq'}, dimensions={0}, use_global_device_ids=true | all-gather | bytes 983040 | tf_op jit(solution)/shard_map/all_gather | solution.py:55
  43.3 2.2 copy.49
  45.5 0.4 fusion.6
  45.8 4.9 %psum.7 = f32[256]{0:T(256)S(1)} all-reduce(f32[256]{0:T(256)S(1)} %fusion.6), channel_id=1, replica_groups=mesh['grp'=2,'slab'=4,'head'=2,'seq'=2] {'head'}, use_global_device_ids=true, to_apply=%region_1.0 | all-reduce | flops 256 | bytes 2048 | tf_op jit(solution)/shard_map/psum | solution.py:41
  50.8 1.7 pad_maximum_fusion
  52.5 0.1 collective-permute-start.2
  52.6 0.4 fusion.8
  53.0 1.2 copy-done.3
  54.2 0.6 multiply_reduce_fusion.1
  54.8 56.9 %collective-permute-done.2 = bf16[256,2560]{0,1:T(8,128)(2,1)} collective-permute-done((bf16[256,2560]{0,1:T(8,128)(2,1)S(1)}, bf16[256,2560]{0,1:T(8,128)(2,1)}, u32[]{:S(2)}, u32[]{:S(2)}) %collective-permute-start.2) | collective-permute-done | bytes 1310752 | tf_op jit(solution)/shard_map/ppermute | solution.py:17
  111.6 9.9 %concatenate.20 = bf16[1024,2560]{0,1:T(8,128)(2,1)} concatenate(bf16[64,2560]{0,1:T(8,128)(2,1)} %copy-done.1, bf16[64,2560]{0,1:T(8,128)(2,1)} %copy-done.2, bf16[128,2560]{0,1:T(8,128)(2,1)} %collective-permute-done.1, bf16[256,2560]{0,1:T(8,128)(2,1)} %collective-permute-done.2, bf16[64,2560]{0,1:T(8,128)(2,1)} %copy-done.1, bf16[64,2560]{0,1:T(8,128)(2,1)} %copy-done.2, ...), dimensions={0} | concatenate | bytes 10485760 | tf_op jit(solution)/shard_map/jit(_roll_dynamic)/concatenate | solution.py:21
  121.5 4.4 %dynamic-slice_select_fusion = bf16[512,2560]{0,1:T(8,128)(2,1)S(1)} fusion(bf16[512,2560]{0,1:T(8,128)(2,1)} %copy.40, bf16[1024,2560]{0,1:T(8,128)(2,1)} %concatenate.20, s32[]{:T(128)S(6)} %select_n.27, pred[]{:T(512)S(6)} %eq.6), kind=kLoop, calls=%fused_computation.15 | loop fusion | flops 1310720 | bytes 7864325 | tf_op jit(solution)/shard_map/jit(_where)/select_n | solution.py:57
  125.9 5.7 %multiply_reduce_fusion = (f32[20,256]{1,0:T(8,128)S(1)}, f32[20,256,512]{2,1,0:T(8,128)}) fusion(bf16[256,20,128]{0,2,1:T(8,128)(2,1)S(1)} %bitcast.25, bf16[512,20,128]{0,2,1:T(8,128)(2,1)S(1)} %bitcast.27), kind=kOutput, calls=%fused_computation.1 | convolution fusion | flops 676326400 | bytes 14438400 | tf_op jit(solution)/shard_map/rhd,khd->hrk/dot_general | solution.py:67
  131.6 20.1 %pmax.7 = f32[20,256]{1,0:T(8,128)S(1)} all-reduce(f32[20,256]{1,0:T(8,128)S(1)} %max.9), channel_id=1, replica_groups=mesh['grp'=2,'slab'=4,'head'=2,'seq'=2] {'slab'}, use_global_device_ids=true, to_apply=%region_4.5 | all-reduce | flops 5120 | bytes 40960 | tf_op jit(solution)/shard_map/pmax | solution.py:84
  151.7 0.5 fusion.9
  152.2 5.8 %fusion = f32[20,256]{1,0:T(8,128)S(1)} fusion(f32[20,256,512]{2,1,0:T(8,128)} %get-tuple-element.8, f32[20,256]{1,0:T(8,128)S(1)} %max.9), kind=kLoop, calls=%fused_computation.2 | loop fusion | flops 7859200 | bytes 10526720 | tf_op jit(solution)/shard_map/reduce_sum | solution.py:76
  158.1 0.8 copy.59
  158.8 0.0 reduce-scatter.10.cloned.1.call-update
  158.8 0.2 reduce-scatter.6.cloned.1.call-start
  159.1 0.0 all-gather.3.cloned.1.call-done
  159.1 4.4 %copy.46 = bf16[512,2560]{0,1:T(8,128)(2,1)} copy(bf16[512,2560]{1,0:T(8,128)(2,1)} %all-gather.3.cloned.1.call-done) | data formatting | bytes 5242880 | tf_op jit(solution)/shard_map/all_gather | solution.py:51
  163.5 2.0 broadcast_select_fusion
  165.5 5.3 %fusion.2 = f32[20,256,128]{2,1,0:T(8,128)S(1)} fusion(bf16[512,20,128]{0,2,1:T(8,128)(2,1)S(1)} %bitcast.26, f32[20,256,512]{2,1,0:T(8,128)} %get-tuple-element.8, f32[20,256]{1,0:T(8,128)S(1)} %max.9), kind=kOutput, calls=%fused_computation.4 | convolution fusion | flops 678952960 | bytes 15749120 | tf_op jit(solution)/shard_map/hrk,khd->hrd/dot_general | solution.py:78
  170.9 2.5 add_multiply_fusion
  173.4 0.0 reduce-scatter.6.cloned.1.call-update
  173.4 0.0 all-gather.5.cloned.1.call-start
  173.5 3.2 %reduce-scatter.10.cloned.1.call-done = f32[64,20]{1,0:T(8,128)} async-done(((f32[256,20]{1,0:T(8,128)}), f32[64,20]{1,0:T(8,128)}) %reduce-scatter.10.cloned.1.call-update) | async-done | bytes 5136
  176.7 0.8 copy.60
  177.5 51.7 %reduce-scatter.6.cloned.1.call-done = f32[20,64,128]{2,1,0:T(8,128)} async-done(((f32[20,256,128]{2,1,0:T(8,128)}), f32[20,64,128]{2,1,0:T(8,128)}) %reduce-scatter.6.cloned.1.call-update) | async-done | bytes 655376 | tf_op jit(solution)/shard_map/reduce_scatter | solution.py:87
  229.2 2.1 divide_convert_fusion
  231.3 0.0 reduce-scatter.8.cloned.1.call-start
  231.3 31.9 %all-gather.5.cloned.1.call-done = bf16[20,256,128]{2,1,0:T(8,128)(2,1)} async-done(((bf16[20,64,128]{2,1,0:T(8,128)(2,1)}), bf16[20,256,128]{2,1,0:T(8,128)(2,1)}) %all-gather.5.cloned.1.call-update) | async-done | bytes 1310736 | tf_op jit(solution)/shard_map/all_gather | solution.py:93
  263.2 6.2 %convolution_bitcast_fusion = f32[256,1280]{1,0:T(8,128)} fusion(bf16[20,256,128]{2,1,0:T(8,128)(2,1)} %all-gather.5.cloned.1.call-done, bf16[20,128,1280]{2,1,0:T(8,128)(2,1)} %bitcast.33), kind=kOutput, calls=%fused_computation.9 | convolution fusion | flops 1677721600 | bytes 9175040 | tf_op jit(solution)/shard_map/hrd,hdc->rc/dot_general | solution.py:95
  270.1 0.4 convolution_reduce_fusion
  270.6 21.4 %reduce-scatter.8.cloned.1.call-done = f32[256,640]{1,0:T(8,128)} async-done(((f32[256,1280]{1,0:T(8,128)}), f32[256,640]{1,0:T(8,128)}) %reduce-scatter.8.cloned.1.call-update) | async-done | bytes 655376 | tf_op jit(solution)/shard_map/reduce_scatter | solution.py:98
  292.0 1.9 multiply_convert_fusion
  (26 shorter events, 0.2 us)
Async XLA Ops:
  7.4 262.8 %copy-start = (f32[256,640]{1,0:T(8,128)S(1)}, f32[256,640]{1,0:T(8,128)}, u32[]{:S(2)}) copy-start(f32[256,640]{1,0:T(8,128)} %param.21) | copy-start | bytes 1966084
  7.4 151.7 %all-gather.3.cloned.1.call-start = ((), (), s32[]{:S(2)}) async-start(), calls=%async_computation.3 | async-start | bytes 2949120 | tf_op jit(solution)/shard_map/all_gather | solution.py:51
  7.4 9.4 %collective-permute-start = (bf16[64,2560]{1,0:T(8,128)(2,1)}, bf16[64,2560]{1,0:T(8,128)(2,1)S(1)}, u32[]{:S(2)}, u32[]{:S(2)}) collective-permute-start(bf16[64,2560]{1,0:T(8,128)(2,1)} %param.16), channel_id=1, source_target_pairs={{0,13},{1,0},{4,1},{5,4},{8,5},{9,8},{12,9},{13,12},{2,15},{3,2},{... | collective-permute-start | bytes 983048 | tf_op jit(solution)/shard_map/ppermute | solution.py:17
  13.2 37.5 %copy-start.1 = (bf16[64,2560]{0,1:T(8,128)(2,1)}, bf16[64,2560]{0,1:T(8,128)(2,1)S(1)}, u32[]{:S(2)}) copy-start(bf16[64,2560]{0,1:T(8,128)(2,1)S(1)} %copy.36) | copy-start | bytes 983044
  17.1 33.6 %copy-start.2 = (bf16[64,2560]{0,1:T(8,128)(2,1)}, bf16[64,2560]{0,1:T(8,128)(2,1)S(1)}, u32[]{:S(2)}) copy-start(bf16[64,2560]{0,1:T(8,128)(2,1)S(1)} %copy.37) | copy-start | bytes 983044
  18.4 32.4 %collective-permute-start.1 = (bf16[128,2560]{0,1:T(8,128)(2,1)}, bf16[128,2560]{0,1:T(8,128)(2,1)}, u32[]{:S(2)}, u32[]{:S(2)}) collective-permute-start(bf16[128,2560]{0,1:T(8,128)(2,1)} %pad_maximum_fusion.1), channel_id=1, source_target_pairs={{0,12},{1,13},{4,0},{5,1},{8,4},{9,5},{12,8},{13,9},{2,14},{3,15},... | collective-permute-start | bytes 1966088 | tf_op jit(solution)/shard_map/ppermute | solution.py:17
  19.0 157.7 %reduce-scatter.10.cloned.1.call-start = ((), (), s32[]{:S(2)}) async-start(), calls=%async_computation.7 | async-start | bytes 163840
  45.5 7.1 %copy-start.7 = (f32[2560]{0:T(1024)S(1)}, f32[2560]{0:T(1024)}, u32[]{:S(2)}) copy-start(f32[2560]{0:T(1024)} %param.13) | copy-start | bytes 30724
  50.8 3.4 %copy-start.6 = (bf16[128,2560]{0,1:T(8,128)(2,1)S(1)}, bf16[128,2560]{0,1:T(8,128)(2,1)}, u32[]{:S(2)}) copy-start(bf16[128,2560]{0,1:T(8,128)(2,1)} %copy.43) | copy-start | bytes 1966084
  52.5 59.1 %collective-permute-start.2 = (bf16[256,2560]{0,1:T(8,128)(2,1)S(1)}, bf16[256,2560]{0,1:T(8,128)(2,1)}, u32[]{:S(2)}, u32[]{:S(2)}) collective-permute-start(bf16[256,2560]{0,1:T(8,128)(2,1)S(1)} %pad_maximum_fusion), channel_id=1, source_target_pairs={{0,8},{1,9},{4,12},{5,13},{8,0},{9,1},{12,4},{13,5},{2,10},{3,11},... | collective-permute-start | bytes 3932168 | tf_op jit(solution)/shard_map/ppermute | solution.py:17
  53.0 1.2 copy-start.3
  121.5 4.4 %copy-start.4 = (bf16[256,2560]{0,1:T(8,128)(2,1)S(1)}, bf16[256,2560]{0,1:T(8,128)(2,1)}, u32[]{:S(2)}) copy-start(bf16[256,2560]{0,1:T(8,128)(2,1)} %copy-done.3) | copy-start | bytes 3932164
  158.8 70.4 %reduce-scatter.6.cloned.1.call-start = ((), (), s32[]{:S(2)}) async-start(), calls=%async_computation.4 | async-start | bytes 3276800 | tf_op jit(solution)/shard_map/reduce_scatter | solution.py:87
  165.5 5.4 %copy-start.5 = (bf16[128,2560]{0,1:T(8,128)(2,1)S(1)}, bf16[128,2560]{0,1:T(8,128)(2,1)}, u32[]{:S(2)}) copy-start(bf16[128,2560]{0,1:T(8,128)(2,1)} %copy.49) | copy-start | bytes 1966084
  173.4 89.8 %all-gather.5.cloned.1.call-start = ((), (), s32[]{:S(2)}) async-start(), calls=%async_computation.5 | async-start | bytes 1638400 | tf_op jit(solution)/shard_map/all_gather | solution.py:93
  231.3 60.7 %reduce-scatter.8.cloned.1.call-start = ((), (), s32[]{:S(2)}) async-start(), calls=%async_computation.6 | async-start | bytes 1966080 | tf_op jit(solution)/shard_map/reduce_scatter | solution.py:98
Sparse Core Ops, SparseCore 0:
  19.1 38.6 all-gather.2
  269.5 22.4 reduce-scatter.7
Sparse Core Ops, SparseCore 1:
  158.9 17.7 reduce-scatter.9
  178.8 50.3 reduce-scatter.5
  231.4 31.8 all-gather.4
